TPU v7x, 32 devices: a whole 2x2x4 slice. The times are simulated.
32 devices in a mesh: groups: 2 (over x), att: 8 (over z, y), exp: 2 (over core).
Axes of the slice: x: 2, y: 2, z: 4, core: 2. Of those that a mesh axis runs over, the one named last changes fastest.
Arguments:
- query: bfloat16 [2048, 2048], P(('groups', 'att'), 'exp'), parts along dimension 0, may hold values from -9 to 9
- new_key: bfloat16 [2048, 256], P(('groups', 'att'), 'exp'), parts along dimension 0, may hold values from -6 to 6
- new_value: bfloat16 [2048, 256], P(('groups', 'att'), 'exp'), parts along dimension 0, may hold values from -6 to 6
- cache_keys: bfloat16 [2048, 64, 256], P(('groups', 'att'), None, 'exp'), parts along dimension 0, may hold values from -9 to 9
- cache_values: bfloat16 [2048, 64, 256], P(('groups', 'att'), None, 'exp'), parts along dimension 0, may hold values from -6 to 6
- lengths: int32 [2048], P(('groups', 'att')), parts along dimension 0, may hold values from 2 to 64, as said below
- out_proj: bfloat16 [2048, 2880], P('exp'), may hold values from -0.125 to 0.125
- residual: bfloat16 [2048, 2880], P(('groups', 'att', 'exp')), parts along dimension 0, may hold values from -6 to 6
- norm_gain: float32 [2880], replicated, may hold values from 0.25 to 1.75
- router: float32 [2880, 8], replicated, may hold values from -0.21875 to 0.21875
- routes: int32 [2048, 4], P(('groups', 'att', 'exp')), parts along dimension 0, may hold values from 0 to 7, all different within a row; in each aligned block of 64 rows (0 to 63, 64 to 127, ...) at most 64 rows name the same one
- w_gate: bfloat16 [8, 2880, 1440], P('att', None, 'exp'), may hold values from -0.109375 to 0.109375
- w_up: bfloat16 [8, 2880, 1440], P('att', None, 'exp'), may hold values from -0.109375 to 0.109375
- w_down: bfloat16 [8, 1440, 2880], P('att', 'exp'), may hold values from -0.15625 to 0.15625
Outputs:
- mixed: bfloat16 [2048, 2880], P(('groups', 'att', 'exp')), parts along dimension 0
There are 2 independent parts, one for each index of `groups`. A program takes and returns all parts, laid end to end along the dimension named above; an argument that names none is the same for every part. Nothing has to cross between parts.
Inputs may be any that keep to these rules, and one draw needn't show every extreme that they name: `routes`: each row names 4 different experts. Among the 64 rows of one device (aligned blocks in order) no expert is named more than 64 times, and that count is reached in every draw. `lengths`: every eighth request, starting with the first, uses all 64 cached positions.
All inputs are finite; a program needn't handle non-finite values.
Results may differ from a plain program's by a relative error of at most 0.0065.
Values may be sent and summed in bfloat16 or wider, within the bound.
A program may use at most 128 MiB of HBM per device.

v0:
```python
import math
import jax
import jax.numpy as jnp
from jax import lax
from jax.sharding import PartitionSpec as P

HEAD = 64


def attend(query, new_key, new_value, cache_keys, cache_values, lengths):
    requests = query.shape[0]
    cache_len = cache_keys.shape[1]
    value_heads = new_key.shape[1] // HEAD
    group_size = query.shape[1] // new_key.shape[1]
    inverse_root = 1.0 / math.sqrt(HEAD)
    queries = query.reshape(requests, value_heads, group_size, HEAD)
    cached_k = cache_keys.reshape(requests, cache_len, value_heads, HEAD)
    cached_v = cache_values.reshape(requests, cache_len, value_heads, HEAD)
    fresh_k = new_key.reshape(requests, value_heads, HEAD)
    fresh_v = new_value.astype(jnp.float32).reshape(requests, value_heads, HEAD)
    cached_scores = (
        jnp.einsum("rjgd,rljd->rjgl", queries, cached_k, preferred_element_type=jnp.float32)
        * inverse_root
    )
    fresh_scores = (
        jnp.einsum("rjgd,rjd->rjg", queries, fresh_k, preferred_element_type=jnp.float32)
        * inverse_root
    )
    live_mask = jnp.arange(cache_len)[None, :] < lengths[:, None]
    cached_scores = jnp.where(live_mask[:, None, None, :], cached_scores, -1e30)
    highest = jnp.maximum(jnp.max(cached_scores, axis=-1), fresh_scores)
    cached_exp = jnp.exp(cached_scores - highest[..., None])
    fresh_exp = jnp.exp(fresh_scores - highest)
    totals = jnp.sum(cached_exp, axis=-1) + fresh_exp
    cached_probs = (cached_exp / totals[..., None]).astype(jnp.bfloat16)
    fresh_probs = (fresh_exp / totals).astype(jnp.bfloat16)
    output = jnp.einsum(
        "rjgl,rljd->rjgd", cached_probs, cached_v, preferred_element_type=jnp.float32
    )
    output = output + fresh_probs.astype(jnp.float32)[..., None] * fresh_v[:, :, None, :]
    return output.astype(jnp.bfloat16).reshape(requests, query.shape[1])


def per_device(
    query,
    new_key,
    new_value,
    cache_keys,
    cache_values,
    lengths,
    out_proj,
    residual,
    norm_gain,
    router,
    routes,
    w_gate,
    w_up,
    w_down,
):
    attended = attend(query, new_key, new_value, cache_keys, cache_values, lengths)
    summed = lax.psum_scatter(
        jnp.dot(attended, out_proj, preferred_element_type=jnp.float32),
        "exp",
        scatter_dimension=0,
        tiled=True,
    )
    hidden_state = residual.astype(jnp.float32) + summed
    mean_square = jnp.mean(hidden_state * hidden_state, axis=-1, keepdims=True)
    normed = (hidden_state * lax.rsqrt(mean_square + 1e-05) * norm_gain).astype(jnp.bfloat16)
    logits = jnp.dot(normed.astype(jnp.float32), router, precision=lax.Precision.HIGHEST)
    chosen_logits = jnp.take_along_axis(logits, routes, axis=1)
    squashed = jax.nn.sigmoid(chosen_logits)
    gate_weights = squashed / jnp.sum(squashed, axis=1, keepdims=True)
    experts = lax.axis_size("att")
    own_rows = routes.shape[0]
    top_count = routes.shape[1]
    width = normed.shape[1]
    capacity = 2 * own_rows * top_count // experts
    flat_routes = routes.reshape(-1)
    onehot = (flat_routes[:, None] == jnp.arange(experts)[None, :]).astype(jnp.int32)
    before = jnp.cumsum(onehot, axis=0) - onehot
    slot_index = jnp.sum(before * onehot, axis=1)
    target = flat_routes * capacity + slot_index
    placing = (jnp.arange(experts * capacity)[:, None] == target[None, :]).reshape(
        experts * capacity, own_rows, top_count
    )
    placing = jnp.any(placing, axis=2).astype(jnp.bfloat16)
    outgoing = jnp.dot(placing, normed, preferred_element_type=jnp.float32).astype(jnp.bfloat16)
    outgoing = outgoing.reshape(experts, capacity, width)
    gate_matrix = w_gate[0]
    up_matrix = w_up[0]
    down_matrix = w_down[0]
    arrived = lax.all_to_all(outgoing, "att", split_axis=0, concat_axis=0, tiled=True)
    routed_block = lax.all_gather(arrived, "exp", axis=1, tiled=True)
    leading = routed_block.shape[:-1]
    flat_rows = routed_block.reshape(-1, routed_block.shape[-1])
    gate_part = jnp.dot(flat_rows, gate_matrix, preferred_element_type=jnp.float32)
    up_part = jnp.dot(flat_rows, up_matrix, preferred_element_type=jnp.float32)
    activated = (jax.nn.silu(gate_part) * up_part).astype(jnp.bfloat16)
    result = jnp.dot(activated, down_matrix, preferred_element_type=jnp.float32)
    partial_value = result.reshape(leading + (result.shape[-1],))
    partial_value = lax.optimization_barrier(partial_value.astype(jnp.bfloat16)).astype(jnp.float32)
    summed_all = lax.psum(partial_value.astype(jnp.bfloat16), "exp").astype(jnp.float32)
    own_block = lax.dynamic_slice_in_dim(summed_all, lax.axis_index("exp") * capacity, capacity, 1)
    finished = own_block.astype(jnp.bfloat16)
    returned = lax.all_to_all(finished, "att", split_axis=0, concat_axis=0, tiled=True)
    flat_back = returned.reshape(-1, returned.shape[-1])
    picked = jnp.take(flat_back, target, axis=0).astype(jnp.float32)
    picked = picked.reshape(own_rows, top_count, returned.shape[-1])
    combined = jnp.sum(picked * gate_weights[:, :, None], axis=1)
    return (hidden_state + combined).astype(jnp.bfloat16)


def solution(mesh):
    in_specs = (
        P(("groups", "att"), "exp"),
        P(("groups", "att"), "exp"),
        P(("groups", "att"), "exp"),
        P(("groups", "att"), None, "exp"),
        P(("groups", "att"), None, "exp"),
        P(("groups", "att")),
        P("exp", None),
        P(("groups", "att", "exp"), None),
        P(),
        P(),
        P(("groups", "att", "exp"), None),
        P("att", None, "exp"),
        P("att", None, "exp"),
        P("att", "exp", None),
    )
    out_specs = P(("groups", "att", "exp"), None)
    return jax.shard_map(
        per_device, mesh=mesh, in_specs=in_specs, out_specs=out_specs, check_vma=False
    )
```

profile of v0, /device:TPU:0, one launch (start us, length us, event | category | flops | bytes accessed | tf_op | source)
XLA Modules:
  0.0 298.4 jit_solution(6635247010307698709)
XLA Ops:
  6.5 3.3 %copy.118 = bf16[128,64,128]{0,2,1:T(8,128)(2,1)S(1)} copy(bf16[128,64,128]{2,1,0:T(8,128)(2,1)} %param.18) | data formatting | bytes 4194304 | tf_op args[4]
  9.9 6.5 %copy.119 = bf16[128,64,2,64]{3,1,2,0:T(8,128)(2,1)} copy(bf16[128,64,2,64]{0,3,2,1:T(8,128)(2,1)S(1)} %bitcast.61) | data formatting | bytes 4194304 | tf_op jit(solution)/shard_map/reshape | solution.py:18
  16.4 0.2 copy.109
  16.5 0.4 copy.111
  17.0 3.3 %copy.110 = bf16[128,64,128]{0,2,1:T(8,128)(2,1)S(1)} copy(bf16[128,64,128]{2,1,0:T(8,128)(2,1)} %param.17) | data formatting | bytes 4194304 | tf_op args[3]
  20.3 6.5 %copy.112 = bf16[128,64,2,64]{3,1,2,0:T(8,128)(2,1)} copy(bf16[128,64,2,64]{0,3,2,1:T(8,128)(2,1)S(1)} %bitcast.62) | data formatting | bytes 4194304 | tf_op jit(solution)/shard_map/reshape | solution.py:17
  26.9 0.1 copy.121
  27.0 0.1 copy.122
  27.2 4.6 %fusion.25 = (f32[128,2,8]{2,1,0:T(2,128)S(1)}, f32[128,2,8,64]{3,2,1,0:T(8,128)S(1)}) fusion(bf16[128,2,8,64]{3,2,1,0:T(8,128)(2,1)S(1)} %copy.111, bf16[128,64,2,64]{3,1,2,0:T(8,128)(2,1)} %copy.112, pred[128,64]{1,0:T(8,128)(4,1)S(1)} %iota_compare_fusion.1), kind=kOutput, calls=%fused_computation.57 | convolution fusion | flops 17168384 | bytes 2899968 | tf_op jit(solution)/shard_map/rjgd,rljd->rjgl/dot_general | solution.py:22
  31.9 0.1 copy.113
  32.1 0.1 copy.115
  32.3 0.8 fusion.14
  33.1 0.2 copy.120
  33.3 0.1 copy.117
  33.4 3.5 %fusion.13 = bf16[128,2,8,64]{3,2,1,0:T(8,128)(2,1)S(1)} fusion(bf16[128,64,2,64]{3,1,2,0:T(8,128)(2,1)} %copy.119, f32[128,2,8,64]{3,2,1,0:T(8,128)S(1)} %get-tuple-element.10, f32[128,2,64]{2,1,0:T(2,128)S(1)} %copy.122, f32[128,2,8]{2,1,0:T(2,128)S(1)} %copy.120, f32[128,2,8]{2,1,0:T(2,128)S(1)} %copy.117, f32[128,2,8]{2,1,0:T(2,128)S(1)} %copy.115), kind=kOutput, calls=%fused_computation.18 | convolution fusion | flops 17563648 | bytes 2973696 | tf_op jit(solution)/shard_map/rjgl,rljd->rjgd/dot_general | solution.py:37
  37.0 0.5 copy.123
  37.5 6.0 %fusion.26 = f32[128,2880]{1,0:T(8,128)} fusion(bf16[128,1024]{0,1:T(8,128)(2,1)S(1)} %bitcast.64, bf16[1024,2880]{0,1:T(8,128)(2,1)} %param.20), kind=kOutput, calls=%fused_computation.58 | convolution fusion | flops 754974720 | bytes 7634944 | tf_op jit(solution)/shard_map/dot_general | solution.py:62
  43.6 0.2 all-gather.2.cloned.1.call-start
  43.9 0.1 eq.40
  44.0 0.1 reshape.164
  44.1 0.6 reduce-window.6
  44.7 0.2 slice_reduce_fusion
  45.1 0.1 reduce_sum.51
  45.3 0.1 fusion.17
  45.4 10.0 %reduce-scatter.2.cloned.1.call-done = f32[64,2880]{1,0:T(8,128)} async-done(((f32[128,2880]{1,0:T(8,128)}), f32[64,2880]{1,0:T(8,128)}) %reduce-scatter.2.cloned.1.call-update) | async-done | bytes 737296 | tf_op jit(solution)/shard_map/reduce_scatter | solution.py:61
  55.4 1.3 multiply_reduce_fusion.1
  56.8 1.3 multiply_convert_fusion.1
  58.0 1.0 convolution_convert_fusion.1
  59.0 3.0 copy.128
  62.0 74.5 %all_to_all.10 = bf16[8,64,2880]{2,1,0:T(8,128)(2,1)} all-to-all(bf16[8,64,2880]{2,1,0:T(8,128)(2,1)} %bitcast.60), channel_id=1, replica_groups=mesh['groups'=2,'att'=8,'exp'=2] {'att'}, dimensions={0} | all-to-all | bytes 5898240 | tf_op jit(solution)/shard_map/all_to_all | solution.py:93
  136.6 15.1 %all-gather.2.cloned.1.call-done = bf16[8,128,2880]{2,1,0:T(8,128)(2,1)} async-done(((bf16[8,64,2880]{2,1,0:T(8,128)(2,1)}), bf16[8,128,2880]{2,1,0:T(8,128)(2,1)}) %all-gather.2.cloned.1.call-update) | async-done | bytes 5898256 | tf_op jit(solution)/shard_map/all_gather | solution.py:94
  151.8 8.2 %fusion.1 = f32[1024,720]{0,1:T(8,128)S(1)} fusion(bf16[1024,2880]{1,0:T(8,128)(2,1)} %bitcast.68, bf16[1,2880,720]{1,2,0:T(8,128)(2,1)} %param.26), kind=kOutput, calls=%fused_computation.6 | convolution fusion | flops 4246732800 | bytes 12994560 | tf_op jit(solution)/shard_map/dot_general | solution.py:98
  160.0 5.2 %fusion.9 = bf16[90,8,8,128]{3,2,1,0:T(8,128)(2,1)S(1)} fusion(f32[1024,720]{0,1:T(8,128)S(1)} %fusion.1, bf16[1024,2880]{1,0:T(8,128)(2,1)S(1)} %bitcast.69, bf16[1,2880,720]{1,2,0:T(8,128)(2,1)S(1)} %bitcast.71), kind=kOutput, calls=%fused_computation.14 | convolution fusion | flops 4251156480 | bytes 14469120 | tf_op jit(solution)/shard_map/dot_general | solution.py:97
  165.3 7.1 %convolution_convert_fusion = bf16[8,128,2880]{2,1,0:T(8,128)(2,1)} fusion(bf16[1,720,2880]{2,1,0:T(8,128)(2,1)S(1)} %bitcast.73, bf16[90,8,8,128]{3,2,1,0:T(8,128)(2,1)S(1)} %fusion.9), kind=kOutput, calls=%fused_computation.3 | convolution fusion | flops 4249681920 | bytes 11520000 | tf_op jit(solution)/shard_map/dot_general | solution.py:100
  172.4 32.2 %all-reduce.2.cloned.1.call-done = bf16[8,128,2880]{2,1,0:T(8,128)(2,1)} async-done(((bf16[8,128,2880]{2,1,0:T(8,128)(2,1)}), bf16[8,128,2880]{2,1,0:T(8,128)(2,1)}) %all-reduce.2.cloned.1.call-update) | async-done | bytes 5898256 | tf_op jit(solution)/shard_map/psum | solution.py:103
  204.6 3.7 %convert_convert_fusion = bf16[8,64,2880]{2,1,0:T(8,128)(2,1)} fusion(bf16[8,128,2880]{2,1,0:T(8,128)(2,1)} %all-reduce.2.cloned.1.call-done, s32[]{:T(128)S(6)} %select_n.41), kind=kLoop, calls=%fused_computation.2 | loop fusion | flops 2949120 | bytes 5898244 | tf_op jit(solution)/shard_map/convert_element_type | solution.py:105
  208.3 5.8 %all-to-all-start.1 = ((bf16[8,64,2880]{2,1,0:T(8,128)(2,1)}), bf16[8,64,2880]{2,1,0:T(8,128)(2,1)S(1)}, u32[]{:S(2)}, u32[]{:S(2)}) async-start(bf16[8,64,2880]{2,1,0:T(8,128)(2,1)} %convert_convert_fusion), calls=%async_computation.2 | async-start | bytes 6029312 | tf_op jit(solution)/shard_map/all_to_all | solution.py:106
  214.2 0.1 reshape.179
  214.4 0.1 mul.113
  214.5 0.1 copy.127
  214.7 0.4 fusion.27
  215.1 1.5 gather_fusion.1
  216.5 0.1 reshape.182
  216.9 65.6 %all-to-all-done.1 = bf16[8,64,2880]{2,1,0:T(8,128)(2,1)S(1)} async-done(((bf16[8,64,2880]{2,1,0:T(8,128)(2,1)}), bf16[8,64,2880]{2,1,0:T(8,128)(2,1)S(1)}, u32[]{:S(2)}, u32[]{:S(2)}) %all-to-all-start.1) | async-done | bytes 2949152 | tf_op jit(solution)/shard_map/all_to_all | solution.py:106
  282.4 2.7 gather_fusion
  285.1 2.9 gather.11
  288.0 3.0 %multiply_reduce_fusion = f32[64,2880]{1,0:T(8,128)S(1)} fusion(f32[64,4]{1,0:T(8,128)S(1)} %copy.134, bf16[64,4,2880]{2,1,0:T(4,128)(2,1)S(1)} %gather.11, pred[64,4]{1,0:T(8,128)(4,1)S(1)} %copy.127), kind=kLoop, calls=%fused_computation.10 | loop fusion | flops 2764800 | bytes 2213120 | tf_op jit(solution)/shard_map/reduce_sum | solution.py:110
  291.1 0.8 add_convert_fusion
  (62 shorter events, 1.2 us)
Async XLA Ops:
  6.5 208.1 %copy-start = (f32[2880,8]{0,1:T(8,128)S(1)}, f32[2880,8]{0,1:T(8,128)}, u32[]{:S(2)}) copy-start(f32[2880,8]{0,1:T(8,128)} %param.23) | copy-start | bytes 276484
  6.5 48.9 %reduce-scatter.2.cloned.1.call-start = ((), (), s32[]{:S(2)}) async-start(), calls=%async_computation.3 | async-start | bytes 2260992 | tf_op jit(solution)/shard_map/reduce_scatter | solution.py:61
  9.9 6.5 %copy-start.4 = (bf16[128,1024]{1,0:T(8,128)(2,1)S(1)}, bf16[128,1024]{1,0:T(8,128)(2,1)}, u32[]{:S(2)}) copy-start(bf16[128,1024]{1,0:T(8,128)(2,1)} %param.14) | copy-start | bytes 786436
  20.3 6.5 %copy-start.9 = (s32[128]{0:T(128)S(1)}, s32[128]{0:T(128)}, u32[]{:S(2)}) copy-start(s32[128]{0:T(128)} %param.19) | copy-start | bytes 1540
  20.3 6.6 %copy-start.6 = (bf16[128,128]{1,0:T(8,128)(2,1)S(1)}, bf16[128,128]{1,0:T(8,128)(2,1)}, u32[]{:S(2)}) copy-start(bf16[128,128]{1,0:T(8,128)(2,1)} %param.16) | copy-start | bytes 98308
  27.2 4.7 %copy-start.7 = (bf16[128,128]{1,0:T(8,128)(2,1)S(1)}, bf16[128,128]{1,0:T(8,128)(2,1)}, u32[]{:S(2)}) copy-start(bf16[128,128]{1,0:T(8,128)(2,1)} %param.15) | copy-start | bytes 98308
  37.5 6.3 %copy-start.5 = (s32[64,4]{0,1:T(4,128)S(1)}, s32[64,4]{0,1:T(4,128)}, u32[]{:S(2)}) copy-start(s32[64,4]{0,1:T(4,128)} %param.24) | copy-start | bytes 3076
  37.5 17.9 %copy-start.2 = (bf16[64,2880]{1,0:T(8,128)(2,1)S(1)}, bf16[64,2880]{1,0:T(8,128)(2,1)}, u32[]{:S(2)}) copy-start(bf16[64,2880]{1,0:T(8,128)(2,1)} %param.21) | copy-start | bytes 1105924
  37.5 19.3 %copy-start.8 = (f32[2880]{0:T(1024)S(1)}, f32[2880]{0:T(1024)}, u32[]{:S(2)}) copy-start(f32[2880]{0:T(1024)} %param.22) | copy-start | bytes 34564
  43.6 108.2 %all-gather.2.cloned.1.call-start = ((), (), s32[]{:S(2)}) async-start(), calls=%async_computation.4 | async-start | bytes 9043968 | tf_op jit(solution)/shard_map/all_gather | solution.py:94
  136.5 23.5 %slice-start = ((s8[4239360]{0:T(1024)(128)(4,1)}), s8[45056]{0:T(1024)(128)(4,1)S(1)}, s32[]{:S(2)}) async-start(s8[4239360]{0:T(1024)(128)(4,1)} %bitcast.70), calls=%async_computation.6 | async-start | bytes 90112
  136.6 68.0 %all-reduce.2.cloned.1.call-start = ((), (), s32[]{:S(2)}) async-start(), calls=%async_computation.5 | async-start | bytes 12058624 | tf_op jit(solution)/shard_map/psum | solution.py:103
  151.8 8.3 %copy-start.10 = (bf16[8,128,2880]{2,1,0:T(8,128)(2,1)S(1)}, bf16[8,128,2880]{2,1,0:T(8,128)(2,1)}, u32[]{:S(2)}) copy-start(bf16[8,128,2880]{2,1,0:T(8,128)(2,1)} %all-gather.2.cloned.1.call-done) | copy-start | bytes 17694724
  151.8 8.3 %slice-start.1 = ((s8[4239360]{0:T(1024)(128)(4,1)}), s8[4194304]{0:T(1024)(128)(4,1)S(1)}, s32[]{:S(2)}) async-start(s8[4239360]{0:T(1024)(128)(4,1)} %bitcast.70), calls=%async_computation.7 | async-start | bytes 8388608
  151.8 13.5 %slice-start.2 = ((s8[4239360]{0:T(1024)(128)(4,1)}), s8[4194304]{0:T(1024)(128)(4,1)S(1)}, s32[]{:S(2)}) async-start(s8[4239360]{0:T(1024)(128)(4,1)} %bitcast.72), calls=%async_computation.8 | async-start | bytes 8388608
  160.0 5.2 %slice-start.3 = ((s8[4239360]{0:T(1024)(128)(4,1)}), s8[45056]{0:T(1024)(128)(4,1)S(1)}, s32[]{:S(2)}) async-start(s8[4239360]{0:T(1024)(128)(4,1)} %bitcast.72), calls=%async_computation.9 | async-start | bytes 90112
  208.3 74.1 %all-to-all-start.1 = ((bf16[8,64,2880]{2,1,0:T(8,128)(2,1)}), bf16[8,64,2880]{2,1,0:T(8,128)(2,1)S(1)}, u32[]{:S(2)}, u32[]{:S(2)}) async-start(bf16[8,64,2880]{2,1,0:T(8,128)(2,1)} %convert_convert_fusion), calls=%async_computation.2 | async-start | bytes 6029312 | tf_op jit(solution)/shard_map/all_to_all | solution.py:106
  285.1 5.9 %copy-start.1 = (f32[64,2880]{1,0:T(8,128)S(1)}, f32[64,2880]{1,0:T(8,128)}, u32[]{:S(2)}) copy-start(f32[64,2880]{1,0:T(8,128)} %reduce-scatter.2.cloned.1.call-done) | copy-start | bytes 2211844
  285.1 5.9 %copy-start.3 = (bf16[64,2880]{1,0:T(8,128)(2,1)S(1)}, bf16[64,2880]{1,0:T(8,128)(2,1)}, u32[]{:S(2)}) copy-start(bf16[64,2880]{1,0:T(8,128)(2,1)} %param.21) | copy-start | bytes 1105924
Sparse Core Ops, SparseCore 0:
  43.7 11.6 reduce-scatter.1
  136.7 15.0 all-gather.1
  172.5 31.9 all-reduce.1
where the time goes:
time: 299 us; the launch traced here: 298 us
  waiting for transfers between devices  123 us (41%)
  blocking collectives  74.5 us (25%)
  matrix products  36.1 us (12%)
  local copies, waits for them, and re-layouts  33.2 us (11%)
  between operations  13.6 us (5%)
  other arithmetic  12.1 us (4%)
  starting transfers between devices  6.05 us (2%)
    all_to_all x1, blocking collectives, per_device(): lax.all_to_all(outgoing, 'att', split_axis=0, concat_axis=0, tiled=True)  74.5 us
    all_to_all x1, waiting for transfers between devices, per_device(): lax.all_to_all(finished, 'att', split_axis=0, concat_axis=0, tiled=True)  65.6 us
    psum x1, waiting for transfers between devices, per_device(): lax.psum(partial_value.astype(jnp.bfloat16), 'exp').astype(jnp.float32)  32.2 us
    all_gather x1, waiting for transfers between devices, per_device(): routed_block = lax.all_gather(arrived, 'exp', axis=1, tiled=True)  15.1 us
    reduce_scatter x1, waiting for transfers between devices, per_device(): lax.psum_scatter(jnp.dot(attended, out_proj, preferred_element_type=jnp.f...  10 us
    dot_general x1, matrix products, per_device(): up_part = jnp.dot(flat_rows, up_matrix, preferred_element_type=jnp.float32)  8.23 us
    unnamed x36, local copies, waits for them, and re-layouts  7.23 us
    dot_general x1, matrix products, per_device(): result = jnp.dot(activated, down_matrix, preferred_element_type=jnp.float32)  7.08 us
  transfers between devices with their start and end apart: 4, of which 4 were waited for; matrix products, arithmetic and copies ran while one was open for 1% of the time, Pallas kernels for 0%

commit v1 on v0

--- a/solution.py
+++ b/solution.py
@@ -100,7 +100,9 @@
     result = jnp.dot(activated, down_matrix, preferred_element_type=jnp.float32)
     partial_value = result.reshape(leading + (result.shape[-1],))
     partial_value = lax.optimization_barrier(partial_value.astype(jnp.bfloat16)).astype(jnp.float32)
-    summed_all = lax.psum(partial_value.astype(jnp.bfloat16), "exp").astype(jnp.float32)
+    summed_all = jnp.sum(lax.all_gather(partial_value.astype(jnp.bfloat16), "exp"), axis=0).astype(
+        jnp.float32
+    )
     own_block = lax.dynamic_slice_in_dim(summed_all, lax.axis_index("exp") * capacity, capacity, 1)
     finished = own_block.astype(jnp.bfloat16)
     returned = lax.all_to_all(finished, "att", split_axis=0, concat_axis=0, tiled=True)

time: 299 us -> 313 us (1.047)
  local copies, waits for them, and re-layouts: 33.2 us -> 45.3 us
  other arithmetic: 12.1 us -> 21.2 us
  waiting for transfers between devices: 123 us -> 116 us
    psum x1 -> x0, waiting for transfers between devices: 32.2 us -> none  [per_device(): lax.psum(partial_value.astype(jnp.bfloat16), 'exp').astype(jnp.float32)]
    all_gather x0 -> x1, waiting for transfers between devices: none -> 25.2 us  [per_device(): lax.all_gather(partial_value.astype(jnp.bfloat16), 'exp')]
    reduce_sum x0 -> x1, other arithmetic: none -> 11 us  [per_device(): jnp.sum(lax.all_gather(partial_value.astype(jnp.bfloat16), 'exp'), axis=0)]
    dynamic_slice x0 -> x1, local copies, waits for them, and re-layouts: none -> 6.82 us  [per_device(): lax.dynamic_slice_in_dim(summed_all, lax.axis_index('exp') * capacity, ca...]
    unnamed x36 -> x37, local copies, waits for them, and re-layouts: 7.23 us -> 12.6 us
where the time goes in v1:
time: 313 us; the launch traced here: 312 us
  waiting for transfers between devices  116 us (37%)
  blocking collectives  74.5 us (24%)
  local copies, waits for them, and re-layouts  45.3 us (14%)
  matrix products  35.8 us (11%)
  other arithmetic  21.2 us (7%)
  between operations  13.6 us (4%)
  starting transfers between devices  6.05 us (2%)
    all_to_all x1, blocking collectives, per_device(): lax.all_to_all(outgoing, 'att', split_axis=0, concat_axis=0, tiled=True)  74.5 us
    all_to_all x1, waiting for transfers between devices, per_device(): lax.all_to_all(finished, 'att', split_axis=0, concat_axis=0, tiled=True)  65.6 us
    all_gather x1, waiting for transfers between devices, per_device(): lax.all_gather(partial_value.astype(jnp.bfloat16), 'exp')  25.2 us
    all_gather x1, waiting for transfers between devices, per_device(): routed_block = lax.all_gather(arrived, 'exp', axis=1, tiled=True)  15.1 us
    unnamed x37, local copies, waits for them, and re-layouts  12.6 us
    reduce_sum x1, other arithmetic, per_device(): jnp.sum(lax.all_gather(partial_value.astype(jnp.bfloat16), 'exp'), axis=0)  11 us
    reduce_scatter x1, waiting for transfers between devices, per_device(): lax.psum_scatter(jnp.dot(attended, out_proj, preferred_element_type=jnp.f...  10 us
    dot_general x1, matrix products, per_device(): up_part = jnp.dot(flat_rows, up_matrix, preferred_element_type=jnp.float32)  8.23 us
  transfers between devices with their start and end apart: 4, of which 4 were waited for; matrix products, arithmetic and copies ran while one was open for 1% of the time, Pallas kernels for 0%

profile of v1, /device:TPU:0, one launch (start us, length us, event | category | flops | bytes accessed | tf_op | source)
XLA Modules:
  0.0 312.5 jit_solution(11227837468834344853)
XLA Ops:
  6.5 3.3 %copy.138 = bf16[128,64,128]{0,2,1:T(8,128)(2,1)S(1)} copy(bf16[128,64,128]{2,1,0:T(8,128)(2,1)} %param.18) | data formatting | bytes 4194304 | tf_op args[4]
  9.9 6.5 %copy.139 = bf16[128,64,2,64]{3,1,2,0:T(8,128)(2,1)} copy(bf16[128,64,2,64]{0,3,2,1:T(8,128)(2,1)S(1)} %bitcast.63) | data formatting | bytes 4194304 | tf_op jit(solution)/shard_map/reshape | solution.py:18
  16.4 0.2 copy.129
  16.5 0.4 copy.131
  17.0 3.3 %copy.130 = bf16[128,64,128]{0,2,1:T(8,128)(2,1)S(1)} copy(bf16[128,64,128]{2,1,0:T(8,128)(2,1)} %param.17) | data formatting | bytes 4194304 | tf_op args[3]
  20.3 6.5 %copy.132 = bf16[128,64,2,64]{3,1,2,0:T(8,128)(2,1)} copy(bf16[128,64,2,64]{0,3,2,1:T(8,128)(2,1)S(1)} %bitcast.64) | data formatting | bytes 4194304 | tf_op jit(solution)/shard_map/reshape | solution.py:17
  26.9 0.1 copy.141
  27.0 0.1 copy.142
  27.2 4.6 %fusion.25 = (f32[128,2,8]{2,1,0:T(2,128)S(1)}, f32[128,2,8,64]{3,2,1,0:T(8,128)S(1)}) fusion(bf16[128,2,8,64]{3,2,1,0:T(8,128)(2,1)S(1)} %copy.131, bf16[128,64,2,64]{3,1,2,0:T(8,128)(2,1)} %copy.132, pred[128,64]{1,0:T(8,128)(4,1)S(1)} %iota_compare_fusion.1), kind=kOutput, calls=%fused_computation.58 | convolution fusion | flops 17168384 | bytes 2899968 | tf_op jit(solution)/shard_map/rjgd,rljd->rjgl/dot_general | solution.py:22
  31.9 0.1 copy.133
  32.1 0.1 copy.135
  32.3 0.8 fusion.14
  33.1 0.2 copy.140
  33.3 0.1 copy.137
  33.4 3.5 %fusion.13 = bf16[128,2,8,64]{3,2,1,0:T(8,128)(2,1)S(1)} fusion(bf16[128,64,2,64]{3,1,2,0:T(8,128)(2,1)} %copy.139, f32[128,2,8,64]{3,2,1,0:T(8,128)S(1)} %get-tuple-element.10, f32[128,2,64]{2,1,0:T(2,128)S(1)} %copy.142, f32[128,2,8]{2,1,0:T(2,128)S(1)} %copy.140, f32[128,2,8]{2,1,0:T(2,128)S(1)} %copy.137, f32[128,2,8]{2,1,0:T(2,128)S(1)} %copy.135), kind=kOutput, calls=%fused_computation.18 | convolution fusion | flops 17563648 | bytes 2973696 | tf_op jit(solution)/shard_map/rjgl,rljd->rjgd/dot_general | solution.py:37
  37.0 0.5 copy.143
  37.5 6.0 %fusion.26 = f32[128,2880]{1,0:T(8,128)} fusion(bf16[128,1024]{0,1:T(8,128)(2,1)S(1)} %bitcast.66, bf16[1024,2880]{0,1:T(8,128)(2,1)} %param.20), kind=kOutput, calls=%fused_computation.59 | convolution fusion | flops 754974720 | bytes 7634944 | tf_op jit(solution)/shard_map/dot_general | solution.py:62
  43.6 0.2 all-gather.4.cloned.1.call-start
  43.9 0.1 eq.40
  44.0 0.1 reshape.164
  44.1 0.6 reduce-window.6
  44.7 0.2 slice_reduce_fusion
  45.1 0.1 reduce_sum.63
  45.3 0.1 fusion.17
  45.4 10.0 %reduce-scatter.2.cloned.1.call-done = f32[64,2880]{1,0:T(8,128)} async-done(((f32[128,2880]{1,0:T(8,128)}), f32[64,2880]{1,0:T(8,128)}) %reduce-scatter.2.cloned.1.call-update) | async-done | bytes 737296 | tf_op jit(solution)/shard_map/reduce_scatter | solution.py:61
  55.4 1.3 multiply_reduce_fusion.1
  56.8 1.3 multiply_convert_fusion.1
  58.0 1.0 convolution_convert_fusion.1
  59.0 3.0 copy.148
  62.0 74.5 %all_to_all.10 = bf16[8,64,2880]{2,1,0:T(8,128)(2,1)} all-to-all(bf16[8,64,2880]{2,1,0:T(8,128)(2,1)} %bitcast.61), channel_id=1, replica_groups=mesh['groups'=2,'att'=8,'exp'=2] {'att'}, dimensions={0} | all-to-all | bytes 5898240 | tf_op jit(solution)/shard_map/all_to_all | solution.py:93
  136.6 15.1 %all-gather.4.cloned.1.call-done = bf16[8,128,2880]{2,1,0:T(8,128)(2,1)} async-done(((bf16[8,64,2880]{2,1,0:T(8,128)(2,1)}), bf16[8,128,2880]{2,1,0:T(8,128)(2,1)}) %all-gather.4.cloned.1.call-update) | async-done | bytes 5898256 | tf_op jit(solution)/shard_map/all_gather | solution.py:94
  151.8 8.2 %fusion.1 = f32[1024,720]{0,1:T(8,128)S(1)} fusion(bf16[1024,2880]{1,0:T(8,128)(2,1)} %bitcast.70, bf16[1,2880,720]{1,2,0:T(8,128)(2,1)} %param.26), kind=kOutput, calls=%fused_computation.6 | convolution fusion | flops 4246732800 | bytes 12994560 | tf_op jit(solution)/shard_map/dot_general | solution.py:98
  160.0 5.2 %fusion.9 = bf16[90,8,8,128]{3,2,1,0:T(8,128)(2,1)S(1)} fusion(f32[1024,720]{0,1:T(8,128)S(1)} %fusion.1, bf16[1024,2880]{1,0:T(8,128)(2,1)S(1)} %bitcast.71, bf16[1,2880,720]{1,2,0:T(8,128)(2,1)S(1)} %bitcast.73), kind=kOutput, calls=%fused_computation.14 | convolution fusion | flops 4251156480 | bytes 14469120 | tf_op jit(solution)/shard_map/dot_general | solution.py:97
  165.3 6.8 %convolution_convert_fusion = bf16[8,128,2880]{1,2,0:T(8,128)(2,1)} fusion(bf16[1,720,2880]{2,1,0:T(8,128)(2,1)S(1)} %bitcast.75, bf16[90,8,8,128]{3,2,1,0:T(8,128)(2,1)S(1)} %fusion.9), kind=kOutput, calls=%fused_computation.3 | convolution fusion | flops 4249681920 | bytes 11520000 | tf_op jit(solution)/shard_map/dot_general | solution.py:100
  172.1 25.2 %all-gather.6.cloned.1.call-done = bf16[16,128,2880]{1,2,0:T(8,128)(2,1)} async-done(((bf16[8,128,2880]{1,2,0:T(8,128)(2,1)}), bf16[16,128,2880]{1,2,0:T(8,128)(2,1)}) %all-gather.6.cloned.1.call-update) | async-done | bytes 11796496 | tf_op jit(solution)/shard_map/all_gather | solution.py:103
  197.3 11.0 %reduce_sum.65 = bf16[8,128,2880]{1,2,0:T(8,128)(2,1)} reduce(bf16[2,8,128,2880]{2,3,1,0:T(8,128)(2,1)} %bitcast.62, bf16[]{:T(256)} %constant.60.clone.1), dimensions={0}, to_apply=%region_8.9 | reduce | flops 2949120 | bytes 17694722 | tf_op jit(solution)/shard_map/reduce_sum | solution.py:103
  208.3 6.8 %constant_dynamic-slice_fusion = bf16[8,64,2880]{1,2,0:T(8,128)(2,1)} fusion(bf16[8,128,2880]{1,2,0:T(8,128)(2,1)} %reduce_sum.65, s32[]{:T(128)S(6)} %select_n.41), kind=kLoop, calls=%fused_computation.55 | loop fusion | bytes 5898244 | tf_op jit(solution)/shard_map/dynamic_slice | solution.py:106
  215.2 5.3 %copy.162 = bf16[8,64,2880]{2,1,0:T(8,128)(2,1)S(1)} copy(bf16[8,64,2880]{1,2,0:T(8,128)(2,1)} %constant_dynamic-slice_fusion) | data formatting | bytes 5898240
  220.5 1.9 convert_convert_fusion
  222.4 5.8 %all-to-all-start.1 = ((bf16[8,64,2880]{2,1,0:T(8,128)(2,1)}), bf16[8,64,2880]{2,1,0:T(8,128)(2,1)S(1)}, u32[]{:S(2)}, u32[]{:S(2)}) async-start(bf16[8,64,2880]{2,1,0:T(8,128)(2,1)} %convert_convert_fusion), calls=%async_computation.2 | async-start | bytes 6029312 | tf_op jit(solution)/shard_map/all_to_all | solution.py:108
  228.6 0.1 copy.147
  228.7 0.4 fusion.27
  229.1 1.5 gather_fusion.1
  230.9 65.6 %all-to-all-done.1 = bf16[8,64,2880]{2,1,0:T(8,128)(2,1)S(1)} async-done(((bf16[8,64,2880]{2,1,0:T(8,128)(2,1)}), bf16[8,64,2880]{2,1,0:T(8,128)(2,1)S(1)}, u32[]{:S(2)}, u32[]{:S(2)}) %all-to-all-start.1) | async-done | bytes 2949152 | tf_op jit(solution)/shard_map/all_to_all | solution.py:108
  296.5 2.7 gather_fusion
  299.2 2.9 gather.11
  302.1 3.0 multiply_reduce_fusion
  305.1 0.8 add_convert_fusion
  (65 shorter events, 1.6 us)
Async XLA Ops:
  6.5 222.2 %copy-start = (f32[2880,8]{0,1:T(8,128)S(1)}, f32[2880,8]{0,1:T(8,128)}, u32[]{:S(2)}) copy-start(f32[2880,8]{0,1:T(8,128)} %param.23) | copy-start | bytes 276484
  6.5 48.9 %reduce-scatter.2.cloned.1.call-start = ((), (), s32[]{:S(2)}) async-start(), calls=%async_computation.3 | async-start | bytes 2260992 | tf_op jit(solution)/shard_map/reduce_scatter | solution.py:61
  9.9 6.5 %copy-start.4 = (bf16[128,1024]{1,0:T(8,128)(2,1)S(1)}, bf16[128,1024]{1,0:T(8,128)(2,1)}, u32[]{:S(2)}) copy-start(bf16[128,1024]{1,0:T(8,128)(2,1)} %param.14) | copy-start | bytes 786436
  20.3 6.5 %copy-start.9 = (s32[128]{0:T(128)S(1)}, s32[128]{0:T(128)}, u32[]{:S(2)}) copy-start(s32[128]{0:T(128)} %param.19) | copy-start | bytes 1540
  20.3 6.6 %copy-start.6 = (bf16[128,128]{1,0:T(8,128)(2,1)S(1)}, bf16[128,128]{1,0:T(8,128)(2,1)}, u32[]{:S(2)}) copy-start(bf16[128,128]{1,0:T(8,128)(2,1)} %param.16) | copy-start | bytes 98308
  27.2 4.7 %copy-start.7 = (bf16[128,128]{1,0:T(8,128)(2,1)S(1)}, bf16[128,128]{1,0:T(8,128)(2,1)}, u32[]{:S(2)}) copy-start(bf16[128,128]{1,0:T(8,128)(2,1)} %param.15) | copy-start | bytes 98308
  37.5 6.3 %copy-start.5 = (s32[64,4]{0,1:T(4,128)S(1)}, s32[64,4]{0,1:T(4,128)}, u32[]{:S(2)}) copy-start(s32[64,4]{0,1:T(4,128)} %param.24) | copy-start | bytes 3076
  37.5 17.9 %copy-start.2 = (bf16[64,2880]{1,0:T(8,128)(2,1)S(1)}, bf16[64,2880]{1,0:T(8,128)(2,1)}, u32[]{:S(2)}) copy-start(bf16[64,2880]{1,0:T(8,128)(2,1)} %param.21) | copy-start | bytes 1105924
  37.5 19.3 %copy-start.8 = (f32[2880]{0:T(1024)S(1)}, f32[2880]{0:T(1024)}, u32[]{:S(2)}) copy-start(f32[2880]{0:T(1024)} %param.22) | copy-start | bytes 34564
  43.6 108.2 %all-gather.4.cloned.1.call-start = ((), (), s32[]{:S(2)}) async-start(), calls=%async_computation.4 | async-start | bytes 9043968 | tf_op jit(solution)/shard_map/all_gather | solution.py:94
  136.5 23.5 %slice-start = ((s8[4239360]{0:T(1024)(128)(4,1)}), s8[45056]{0:T(1024)(128)(4,1)S(1)}, s32[]{:S(2)}) async-start(s8[4239360]{0:T(1024)(128)(4,1)} %bitcast.72), calls=%async_computation.6 | async-start | bytes 90112
  136.6 60.8 %all-gather.6.cloned.1.call-start = ((), (), s32[]{:S(2)}) async-start(), calls=%async_computation.5 | async-start | bytes 17694720 | tf_op jit(solution)/shard_map/all_gather | solution.py:103
  151.8 8.3 %copy-start.10 = (bf16[8,128,2880]{2,1,0:T(8,128)(2,1)S(1)}, bf16[8,128,2880]{2,1,0:T(8,128)(2,1)}, u32[]{:S(2)}) copy-start(bf16[8,128,2880]{2,1,0:T(8,128)(2,1)} %all-gather.4.cloned.1.call-done) | copy-start | bytes 17694724
  151.8 8.3 %slice-start.1 = ((s8[4239360]{0:T(1024)(128)(4,1)}), s8[4194304]{0:T(1024)(128)(4,1)S(1)}, s32[]{:S(2)}) async-start(s8[4239360]{0:T(1024)(128)(4,1)} %bitcast.72), calls=%async_computation.7 | async-start | bytes 8388608
  151.8 13.5 %slice-start.2 = ((s8[4239360]{0:T(1024)(128)(4,1)}), s8[4194304]{0:T(1024)(128)(4,1)S(1)}, s32[]{:S(2)}) async-start(s8[4239360]{0:T(1024)(128)(4,1)} %bitcast.74), calls=%async_computation.8 | async-start | bytes 8388608
  160.0 5.2 %slice-start.3 = ((s8[4239360]{0:T(1024)(128)(4,1)}), s8[45056]{0:T(1024)(128)(4,1)S(1)}, s32[]{:S(2)}) async-start(s8[4239360]{0:T(1024)(128)(4,1)} %bitcast.74), calls=%async_computation.9 | async-start | bytes 90112
  222.4 74.1 %all-to-all-start.1 = ((bf16[8,64,2880]{2,1,0:T(8,128)(2,1)}), bf16[8,64,2880]{2,1,0:T(8,128)(2,1)S(1)}, u32[]{:S(2)}, u32[]{:S(2)}) async-start(bf16[8,64,2880]{2,1,0:T(8,128)(2,1)} %convert_convert_fusion), calls=%async_computation.2 | async-start | bytes 6029312 | tf_op jit(solution)/shard_map/all_to_all | solution.py:108
  299.2 5.9 %copy-start.1 = (f32[64,2880]{1,0:T(8,128)S(1)}, f32[64,2880]{1,0:T(8,128)}, u32[]{:S(2)}) copy-start(f32[64,2880]{1,0:T(8,128)} %reduce-scatter.2.cloned.1.call-done) | copy-start | bytes 2211844
  299.2 5.9 %copy-start.3 = (bf16[64,2880]{1,0:T(8,128)(2,1)S(1)}, bf16[64,2880]{1,0:T(8,128)(2,1)}, u32[]{:S(2)}) copy-start(bf16[64,2880]{1,0:T(8,128)(2,1)} %param.21) | copy-start | bytes 1105924
Sparse Core Ops, SparseCore 0:
  43.7 11.6 reduce-scatter.1
  136.7 15.0 all-gather.3
  172.2 25.0 all-gather.5
